TPU v7x, 32 devices: a whole 2x2x4 slice. The times are simulated.
32 devices in a mesh: section: 4 (over y, x), rows: 2 (over core), dp: 4 (over z).
Axes of the slice: x: 2, y: 2, z: 4, core: 2. Of those that a mesh axis runs over, the one named last changes fastest.
Arguments:
- images: bfloat16 [8, 48, 16, 384], P('dp', 'rows'), may hold values from -6 to 6
- cotangent: bfloat16 [8, 48, 16, 384], P('dp', 'rows'), may hold values from -6 to 6
- order: int32 [4, 2], P('dp'), may hold values from 0 to 1, each once within a row
- heights: int32 [8], P('dp'), may hold values from 12 to 48, as said below
- kernel: float32 [4, 49, 384], P('section'), may hold values from -0.875 to 0.875
- biases: float32 [4, 3, 384], P('section'), may hold values from -3 to 3
- gain: float32 [4, 384], P('section'), may hold values from 0.25 to 1.75
- scale: float32 [4, 384], P('section'), may hold values from 0.4 to 1.2
- up_weight: bfloat16 [4, 384, 1536], P('section'), may hold values from -0.3125 to 0.3125
- up_bias: float32 [4, 1536], P('section'), may hold values from -3 to 3
- down_weight: bfloat16 [4, 1536, 384], P('section'), may hold values from -0.15625 to 0.15625
Outputs:
- kernel_grad: bfloat16 [4, 49, 384], P('section')
- bias_grad: bfloat16 [4, 3, 384], P('section')
- gain_grad: bfloat16 [4, 384], P('section')
- scale_grad: bfloat16 [4, 384], P('section')
- up_weight_grad: bfloat16 [4, 384, 1536], P('section')
- up_bias_grad: bfloat16 [4, 1536], P('section')
- down_weight_grad: bfloat16 [4, 1536, 384], P('section')
Inputs may be any that keep to these rules, and one draw needn't show every extreme that they name: `order`: each row holds every number of 0 to 1 once. `heights`: some image has all 48 rows and some image has 12 rows.
All inputs are finite; a program needn't handle non-finite values.
Results may differ from a plain program's by a relative error of at most 0.015.
Values may be sent and summed in bfloat16 or wider, within the bound.
No kernel may reach another device: no remote copies, remote signals or barrier semaphores. Data moves between devices by JAX's collectives and lax.ppermute only.
A program may use at most 128 MiB of HBM per device.

v0:
```python
import math
import jax
import jax.numpy as jnp
from jax import lax
from jax.sharding import PartitionSpec as P

EPS = 1e-06
ROOT_HALF = 0.7071067811865476
INV_ROOT_TAU = 0.3989422804014327


def extended(block, sides, width):
    for axis, dim in sides:
        count = lax.axis_size(axis)
        forward = [(i, i + 1) for i in range(count - 1)]
        backward = [(target, source) for source, target in forward]
        low = lax.ppermute(
            lax.slice_in_dim(block, block.shape[dim] - width, None, axis=dim), axis, forward
        )
        high = lax.ppermute(lax.slice_in_dim(block, 0, width, axis=dim), axis, backward)
        block = jnp.concatenate([low, block, high], axis=dim)
    return block


def shifted(value, axis, steps):
    count = lax.axis_size(axis)
    leading, last = (max(0, -steps), min(count, count - steps))
    return lax.ppermute(value, axis, [(source, source + steps) for source in range(leading, last)])


def gelu_exact(values):
    return 0.5 * values * (1.0 + lax.erf(values * ROOT_HALF))


def gelu_slope(values):
    return (
        0.5 * (1.0 + lax.erf(values * ROOT_HALF))
        + values * jnp.exp(-0.5 * values * values) * INV_ROOT_TAU
    )


def widen_cols(padded):
    return jnp.pad(padded.astype(jnp.float32), ((0, 0), (3, 3), (0, 0)))


def block_forward(padded, row_mask, params):
    kern, biases, gain, scale, up_weight, up_bias, down_weight = params
    row_count = padded.shape[0] - 6
    col_count = padded.shape[1]
    channels = padded.shape[2]
    field = widen_cols(padded)
    inner = field[3:-3, 3:-3]
    conv = jnp.zeros((row_count, col_count, channels), jnp.float32)
    for i in range(7):
        for j in range(7):
            conv = conv + kern[i * 7 + j] * field[i : i + row_count, j : j + col_count]
    conv = conv + biases[0]
    centred = conv - jnp.mean(conv, axis=-1, keepdims=True)
    inv_std = lax.rsqrt(jnp.mean(centred * centred, axis=-1, keepdims=True) + EPS)
    normed = centred * inv_std
    features = (normed * gain + biases[1]).astype(jnp.bfloat16).reshape(-1, channels)
    hidden_pre = jnp.dot(features, up_weight, preferred_element_type=jnp.float32) + up_bias
    hidden = gelu_exact(hidden_pre).astype(jnp.bfloat16)
    branch = (jnp.dot(hidden, down_weight, preferred_element_type=jnp.float32) + biases[2]).reshape(
        row_count, col_count, channels
    )
    output = (row_mask * (inner + scale * branch)).astype(jnp.bfloat16)
    return (output, (padded, normed, inv_std, features, hidden_pre, branch))


def block_backward_first(grad_out, saved, row_mask, params):
    padded, normed, inv_std, features, hidden_pre, branch = saved
    kern, biases, gain, scale, up_weight, up_bias, down_weight = params
    channels = normed.shape[2]
    grad_res = row_mask * grad_out.astype(jnp.float32)
    scaled = scale * grad_res
    grad_scale = jnp.sum(branch * grad_res, axis=(0, 1))
    grad_bias_out = jnp.sum(scaled, axis=(0, 1))
    grad_branch = scaled.astype(jnp.bfloat16).reshape(-1, channels)
    hidden = gelu_exact(hidden_pre).astype(jnp.bfloat16)
    grad_down = lax.dot_general(
        hidden, grad_branch, (((0,), (0,)), ((), ())), preferred_element_type=jnp.float32
    )
    grad_hidden = lax.dot_general(
        grad_branch, down_weight, (((1,), (1,)), ((), ())), preferred_element_type=jnp.float32
    )
    grad_pre = grad_hidden * gelu_slope(hidden_pre)
    grad_up_bias = jnp.sum(grad_pre, axis=0)
    grad_pre_low = grad_pre.astype(jnp.bfloat16)
    grad_up = lax.dot_general(
        features, grad_pre_low, (((0,), (0,)), ((), ())), preferred_element_type=jnp.float32
    )
    grad_feat = lax.dot_general(
        grad_pre_low, up_weight, (((1,), (1,)), ((), ())), preferred_element_type=jnp.float32
    ).reshape(normed.shape)
    grad_gain = jnp.sum(grad_feat * normed, axis=(0, 1))
    grad_norm_bias = jnp.sum(grad_feat, axis=(0, 1))
    grad_normed = grad_feat * gain
    grad_conv = inv_std * (
        grad_normed
        - jnp.mean(grad_normed, axis=-1, keepdims=True)
        - normed * jnp.mean(grad_normed * normed, axis=-1, keepdims=True)
    )
    grad_conv_bias = jnp.sum(grad_conv, axis=(0, 1))
    small = (
        jnp.stack([grad_conv_bias, grad_norm_bias, grad_bias_out]),
        grad_gain[None],
        grad_scale[None],
        grad_up,
        grad_up_bias[None],
        grad_down,
    )
    return (grad_res, grad_conv, small)


def block_backward_second(grad_res, grad_conv, conv_padded, padded, row_mask, kern):
    row_count = grad_conv.shape[0]
    col_count = grad_conv.shape[1]
    field = widen_cols(padded)
    spread = widen_cols(conv_padded)
    taps = []
    total = jnp.zeros(grad_conv.shape, jnp.float32)
    for i in range(7):
        for j in range(7):
            taps.append(
                jnp.sum(field[i : i + row_count, j : j + col_count] * grad_conv, axis=(0, 1))
            )
            total = (
                total
                + kern[i * 7 + j] * spread[6 - i : 6 - i + row_count, 6 - j : 6 - j + col_count]
            )
    grad_in = (row_mask * (grad_res + total)).astype(jnp.bfloat16)
    return (grad_in, jnp.stack(taps))


def body(
    images, cotangent, order, heights, kernel, biases, gain, scale, up_weight, up_bias, down_weight
):
    section_count = lax.axis_size("section")
    section_at = lax.axis_index("section")
    slot_count, row_count, col_count, channels = images.shape
    hidden_count = up_weight.shape[2]
    first_row = lax.axis_index("rows") * row_count
    lines = first_row + jnp.arange(row_count, dtype=jnp.int32)
    params = (kernel[0], biases[0], gain[0], scale[0], up_weight[0], up_bias[0], down_weight[0])
    tick_list = jnp.arange(slot_count + section_count - 1, dtype=jnp.int32)

    def slot_state(tick_no, lag):
        offset = tick_no - lag
        active = (offset >= 0) & (offset < slot_count)
        slot_at = jnp.clip(offset, 0, slot_count - 1)
        image_at = order[0, slot_at]
        height = heights[image_at]
        row_mask = (lines < height).astype(jnp.float32)[:, None, None]
        has_rows = active & (first_row < height)
        return (slot_at, image_at, row_mask, active, has_rows)

    store_start = (
        jnp.zeros((slot_count, row_count + 6, col_count, channels), jnp.bfloat16),
        jnp.zeros((slot_count, row_count, col_count, channels), jnp.float32),
        jnp.zeros((slot_count, row_count, col_count, 1), jnp.float32),
        jnp.zeros((slot_count, row_count * col_count, channels), jnp.bfloat16),
        jnp.zeros((slot_count, row_count * col_count, hidden_count), jnp.float32),
        jnp.zeros((slot_count, row_count, col_count, channels), jnp.float32),
    )

    def forward_tick(carry, tick_no):
        incoming, stored = carry
        slot_at, image_at, row_mask, active, has_rows = slot_state(tick_no, section_at)
        fresh = jnp.where(row_mask > 0, images[image_at], jnp.zeros((), jnp.bfloat16))
        entering = jnp.where(section_at == 0, fresh, incoming)
        padded = extended(entering, (("rows", 0),), 3)
        result, saved = block_forward(padded, row_mask, params)
        stored = tuple(
            (
                whole.at[slot_at].set(jnp.where(active, piece, whole[slot_at]))
                for whole, piece in zip(stored, saved)
            )
        )
        outgoing = shifted(result, "section", 1)
        return ((outgoing, stored), None)

    blank_act = jnp.zeros((row_count, col_count, channels), jnp.bfloat16)
    stored = lax.scan(forward_tick, (blank_act, store_start), tick_list)[0][1]

    def backward_tick(carry, tick_no):
        incoming, totals = carry
        slot_at, image_at, row_mask, active, has_rows = slot_state(
            tick_no, section_count - 1 - section_at
        )
        grad_out = jnp.where(section_at == section_count - 1, cotangent[slot_at], incoming)
        saved = tuple((whole[slot_at] for whole in stored))
        grad_res, grad_conv, small = block_backward_first(grad_out, saved, row_mask, params)
        conv_padded = extended(grad_conv.astype(jnp.bfloat16), (("rows", 0),), 3).astype(
            grad_conv.dtype
        )
        grad_in, taps = block_backward_second(
            grad_res, grad_conv, conv_padded, saved[0], row_mask, params[0]
        )
        terms = (taps,) + small
        totals = tuple((total + jnp.where(active, term, 0.0) for total, term in zip(totals, terms)))
        outgoing = shifted(grad_in, "section", -1)
        return ((outgoing, totals), None)

    grads_start = (
        jnp.zeros((49, channels), jnp.float32),
        jnp.zeros((3, channels), jnp.float32),
        jnp.zeros((1, channels), jnp.float32),
        jnp.zeros((1, channels), jnp.float32),
        jnp.zeros((channels, hidden_count), jnp.float32),
        jnp.zeros((1, hidden_count), jnp.float32),
        jnp.zeros((hidden_count, channels), jnp.float32),
    )
    totals = lax.scan(backward_tick, (blank_act, grads_start), tick_list)[0][1]
    factor = 1.0 / math.sqrt(
        lax.axis_size("dp") * slot_count * lax.axis_size("rows") * row_count * col_count
    )
    summed = lax.psum(
        (totals[0], totals[1], totals[2], totals[3], totals[4], totals[5], totals[6]),
        ("rows", "dp"),
    )
    finished = tuple(((part * factor).astype(jnp.bfloat16) for part in summed))
    return (
        finished[0][None],
        finished[1][None],
        finished[2],
        finished[3],
        finished[4][None],
        finished[5],
        finished[6][None],
    )


def solution(mesh):
    in_specs = (
        P("dp", "rows", None, None),
        P("dp", "rows", None, None),
        P("dp", None),
        P("dp"),
        P("section", None, None),
        P("section", None, None),
        P("section", None),
        P("section", None),
        P("section", None, None),
        P("section", None),
        P("section", None, None),
    )
    out_specs = (
        P("section", None, None),
        P("section", None, None),
        P("section", None),
        P("section", None),
        P("section", None, None),
        P("section", None),
        P("section", None, None),
    )
    return jax.shard_map(body, mesh=mesh, in_specs=in_specs, out_specs=out_specs, check_vma=False)
```

profile of v0, /device:TPU:0, one launch (start us, length us, event | category | flops | bytes accessed | tf_op | source)
XLA Modules:
  0.0 707.3 jit_solution(5315911890575509953)
XLA Ops:
  10.1 2.7 broadcast_in_dim.122
  17.4 230.1 %while.58 = (s32[]{:T(128)}, bf16[24,16,384]{2,1,0:T(8,128)(2,1)S(1)}, bf16[2,30,16,384]{3,2,1,0:T(8,128)(2,1)}, f32[2,24,16,384]{3,2,1,0:T(8,128)}, f32[2,24,16...) while((s32[]{:T(128)}, ...), condition=%wide.region_5.6_spmd.clone, body=%wide.region_0.5_spmd.clone.sunk | while | flops 930707456 | bytes 118534944 | solution.py:184
  26.7 3.0 collective-permute-start.1
  35.1 1.9 constant_dynamic-slice_fusion.12
  42.0 5.4 fusion.394
  52.5 5.1 collective-permute-start.2
  61.0 2.4 collective-permute-done.2
  72.7 3.0 collective-permute-start.1
  81.2 1.9 constant_dynamic-slice_fusion.12
  88.0 5.4 fusion.394
  98.6 4.7 collective-permute-start.2
  106.6 2.4 collective-permute-done.2
  118.3 3.0 collective-permute-start.1
  126.8 1.9 constant_dynamic-slice_fusion.12
  133.6 5.4 fusion.394
  144.2 4.7 collective-permute-start.2
  152.2 2.4 collective-permute-done.2
  163.9 3.0 collective-permute-start.1
  172.3 1.9 constant_dynamic-slice_fusion.12
  179.2 5.4 fusion.394
  189.8 5.5 collective-permute-start.2
  198.6 2.4 collective-permute-done.2
  210.3 3.0 collective-permute-start.1
  218.7 1.9 constant_dynamic-slice_fusion.12
  225.6 5.4 fusion.394
  236.1 5.6 collective-permute-start.2
  245.1 2.4 collective-permute-done.2
  248.1 328.2 %while.59 = (s32[]{:T(128)}, bf16[24,16,384]{2,1,0:T(8,128)(2,1)S(1)}, f32[49,384]{1,0:T(8,128)}, f32[3,384]{1,0:T(4,128)}, f32[1,384]{1,0:T(1,128)}, /*index=5*...) while((s32[]{:T(128)}, ...), condition=%wide.region_64.65_spmd.clone, body=%wide.region_6.64_spmd.clone.sunk | while | flops 1859761920 | bytes 116535416 | solution.py:214
  256.1 1.9 fusion.408
  258.3 3.3 fusion.410
  265.3 2.4 fusion.413
  267.7 2.2 fusion.414
  272.6 4.2 collective-permute-start.4
  285.7 3.4 fusion.423
  293.4 5.0 fusion.416
  320.9 1.9 fusion.408
  323.0 3.3 fusion.410
  330.1 2.4 fusion.413
  332.5 2.2 fusion.414
  337.3 4.2 collective-permute-start.4
  350.5 3.4 fusion.423
  358.2 5.0 fusion.416
  388.5 3.3 fusion.410
  395.6 2.4 fusion.413
  398.0 2.2 fusion.414
  402.8 4.2 collective-permute-start.4
  416.0 3.4 fusion.423
  423.7 5.0 fusion.416
  451.9 1.9 fusion.408
  454.0 3.3 fusion.410
  461.0 2.4 fusion.413
  463.4 2.2 fusion.414
  468.3 4.2 collective-permute-start.4
  482.1 3.4 fusion.423
  489.8 5.0 fusion.416
  520.1 3.3 fusion.410
  527.2 2.4 fusion.413
  529.6 2.2 fusion.414
  534.4 4.2 collective-permute-start.4
  548.2 3.4 fusion.423
  555.9 5.0 fusion.416
  577.0 28.8 %all-reduce.3 = (f32[3,384]{1,0:T(4,128)S(1)}, f32[1,384]{1,0:T(1,128)S(1)}, f32[1,384]{1,0:T(1,128)S(1)}, f32[1,1536]{1,0:T(1,128)S(1)}) all-reduce(f32[3,384]{1,0:T(4,128)S(1)} %copy-done.39, f32[1,384]{1,0:T(1,128)S(1)} %copy-done.90, f32[1,384]{1,0:T(1,128)S(1)} %copy-done.91, ...), channel_id=1, replica_groups=mesh['section'=4,'rows'=2,'dp'=4] {'rows','dp'}, use_global_device_ids=true, to_apply=%region_66.67 | all-reduce | flops 3456 | bytes 27648 | tf_op jit(solution)/shard_map/psum | solution.py:218
  607.6 88.0 %all-reduce.7.cloned.1.call-done = (f32[49,384]{1,0:T(8,128)}, f32[384,1536]{1,0:T(8,128)}, f32[1536,384]{1,0:T(8,128)}) async-done(((f32[49,384]{1,0:T(8,128)}, f32[384,1536]{1,0:T(8,128)}, f32[1536,384]{1,0:T(8,128)}), (f32[49,384]{1,0:T(8,128)}, f32[384,1536]{1,0:T(8,128)}, f32[1536,384]{1,0:T(8,128)})) %all-reduce.7.cloned.1.call-update) | async-done | bytes 4793872 | tf_op jit(solution)/shard_map/psum | solution.py:218
  695.6 3.0 fusion.334
  (1584 shorter events, 337.8 us)
Async XLA Ops:
  7.2 688.4 %all-reduce.7.cloned.1.call-start = ((), (), s32[]{:S(2)}) async-start(), calls=%async_computation | async-start | bytes 9609216 | tf_op jit(solution)/shard_map/psum | solution.py:218
  25.4 16.5 %collective-permute-start = (bf16[3,16,384]{2,1,0:T(8,128)(2,1)S(1)}, bf16[3,16,384]{2,1,0:T(8,128)(2,1)S(1)}, u32[]{:S(2)}, u32[]{:S(2)}) collective-permute-start(bf16[3,16,384]{2,1,0:T(8,128)(2,1)S(1)} %get-tuple-element.1573), channel_id=1, source_target_pairs={{4,0},{5,1},{6,2},{7,3},{12,8},{13,9},{14,10},{15,11},{20,16},{21,... | collective-permute-start | bytes 110600 | tf_op jit(solution)/shard_map/while/body/eval_jaxpr/ppermute | solution.py:20
  26.7 15.2 %collective-permute-start.1 = (bf16[3,16,384]{2,1,0:T(8,128)(2,1)S(1)}, bf16[3,16,384]{2,1,0:T(8,128)(2,1)S(1)}, u32[]{:S(2)}, u32[]{:S(2)}) collective-permute-start(bf16[3,16,384]{2,1,0:T(8,128)(2,1)S(1)} %get-tuple-element.1574), channel_id=1, source_target_pairs={{0,4},{1,5},{2,6},{3,7},{8,12},{9,13},{10,14},{11,15},{16,20},{17,... | collective-permute-start | bytes 110600 | tf_op jit(solution)/shard_map/while/body/eval_jaxpr/ppermute | solution.py:17
  52.5 10.9 %collective-permute-start.2 = (bf16[24,16,384]{2,1,0:T(8,128)(2,1)S(1)}, bf16[24,16,384]{2,1,0:T(8,128)(2,1)S(1)}, u32[]{:S(2)}, u32[]{:S(2)}) collective-permute-start(bf16[24,16,384]{2,1,0:T(8,128)(2,1)S(1)} %multiply_convert_fusion.15), channel_id=1, source_target_pairs={{0,8},{8,16},{16,24},{1,9},{9,17},{17,25},{2,10},{10,18},{18,26},{... | collective-permute-start | bytes 884744 | tf_op jit(solution)/shard_map/while/body/eval_jaxpr/ppermute | solution.py:28
  71.4 16.5 %collective-permute-start = (bf16[3,16,384]{2,1,0:T(8,128)(2,1)S(1)}, bf16[3,16,384]{2,1,0:T(8,128)(2,1)S(1)}, u32[]{:S(2)}, u32[]{:S(2)}) collective-permute-start(bf16[3,16,384]{2,1,0:T(8,128)(2,1)S(1)} %get-tuple-element.1573), channel_id=1, source_target_pairs={{4,0},{5,1},{6,2},{7,3},{12,8},{13,9},{14,10},{15,11},{20,16},{21,... | collective-permute-start | bytes 110600 | tf_op jit(solution)/shard_map/while/body/eval_jaxpr/ppermute | solution.py:20
  72.7 15.2 %collective-permute-start.1 = (bf16[3,16,384]{2,1,0:T(8,128)(2,1)S(1)}, bf16[3,16,384]{2,1,0:T(8,128)(2,1)S(1)}, u32[]{:S(2)}, u32[]{:S(2)}) collective-permute-start(bf16[3,16,384]{2,1,0:T(8,128)(2,1)S(1)} %get-tuple-element.1574), channel_id=1, source_target_pairs={{0,4},{1,5},{2,6},{3,7},{8,12},{9,13},{10,14},{11,15},{16,20},{17,... | collective-permute-start | bytes 110600 | tf_op jit(solution)/shard_map/while/body/eval_jaxpr/ppermute | solution.py:17
  98.6 10.5 %collective-permute-start.2 = (bf16[24,16,384]{2,1,0:T(8,128)(2,1)S(1)}, bf16[24,16,384]{2,1,0:T(8,128)(2,1)S(1)}, u32[]{:S(2)}, u32[]{:S(2)}) collective-permute-start(bf16[24,16,384]{2,1,0:T(8,128)(2,1)S(1)} %multiply_convert_fusion.15), channel_id=1, source_target_pairs={{0,8},{8,16},{16,24},{1,9},{9,17},{17,25},{2,10},{10,18},{18,26},{... | collective-permute-start | bytes 884744 | tf_op jit(solution)/shard_map/while/body/eval_jaxpr/ppermute | solution.py:28
  117.0 16.5 %collective-permute-start = (bf16[3,16,384]{2,1,0:T(8,128)(2,1)S(1)}, bf16[3,16,384]{2,1,0:T(8,128)(2,1)S(1)}, u32[]{:S(2)}, u32[]{:S(2)}) collective-permute-start(bf16[3,16,384]{2,1,0:T(8,128)(2,1)S(1)} %get-tuple-element.1573), channel_id=1, source_target_pairs={{4,0},{5,1},{6,2},{7,3},{12,8},{13,9},{14,10},{15,11},{20,16},{21,... | collective-permute-start | bytes 110600 | tf_op jit(solution)/shard_map/while/body/eval_jaxpr/ppermute | solution.py:20
  118.3 15.2 %collective-permute-start.1 = (bf16[3,16,384]{2,1,0:T(8,128)(2,1)S(1)}, bf16[3,16,384]{2,1,0:T(8,128)(2,1)S(1)}, u32[]{:S(2)}, u32[]{:S(2)}) collective-permute-start(bf16[3,16,384]{2,1,0:T(8,128)(2,1)S(1)} %get-tuple-element.1574), channel_id=1, source_target_pairs={{0,4},{1,5},{2,6},{3,7},{8,12},{9,13},{10,14},{11,15},{16,20},{17,... | collective-permute-start | bytes 110600 | tf_op jit(solution)/shard_map/while/body/eval_jaxpr/ppermute | solution.py:17
  144.2 10.5 %collective-permute-start.2 = (bf16[24,16,384]{2,1,0:T(8,128)(2,1)S(1)}, bf16[24,16,384]{2,1,0:T(8,128)(2,1)S(1)}, u32[]{:S(2)}, u32[]{:S(2)}) collective-permute-start(bf16[24,16,384]{2,1,0:T(8,128)(2,1)S(1)} %multiply_convert_fusion.15), channel_id=1, source_target_pairs={{0,8},{8,16},{16,24},{1,9},{9,17},{17,25},{2,10},{10,18},{18,26},{... | collective-permute-start | bytes 884744 | tf_op jit(solution)/shard_map/while/body/eval_jaxpr/ppermute | solution.py:28
  162.6 16.5 %collective-permute-start = (bf16[3,16,384]{2,1,0:T(8,128)(2,1)S(1)}, bf16[3,16,384]{2,1,0:T(8,128)(2,1)S(1)}, u32[]{:S(2)}, u32[]{:S(2)}) collective-permute-start(bf16[3,16,384]{2,1,0:T(8,128)(2,1)S(1)} %get-tuple-element.1573), channel_id=1, source_target_pairs={{4,0},{5,1},{6,2},{7,3},{12,8},{13,9},{14,10},{15,11},{20,16},{21,... | collective-permute-start | bytes 110600 | tf_op jit(solution)/shard_map/while/body/eval_jaxpr/ppermute | solution.py:20
  163.9 15.2 %collective-permute-start.1 = (bf16[3,16,384]{2,1,0:T(8,128)(2,1)S(1)}, bf16[3,16,384]{2,1,0:T(8,128)(2,1)S(1)}, u32[]{:S(2)}, u32[]{:S(2)}) collective-permute-start(bf16[3,16,384]{2,1,0:T(8,128)(2,1)S(1)} %get-tuple-element.1574), channel_id=1, source_target_pairs={{0,4},{1,5},{2,6},{3,7},{8,12},{9,13},{10,14},{11,15},{16,20},{17,... | collective-permute-start | bytes 110600 | tf_op jit(solution)/shard_map/while/body/eval_jaxpr/ppermute | solution.py:17
  189.8 11.3 %collective-permute-start.2 = (bf16[24,16,384]{2,1,0:T(8,128)(2,1)S(1)}, bf16[24,16,384]{2,1,0:T(8,128)(2,1)S(1)}, u32[]{:S(2)}, u32[]{:S(2)}) collective-permute-start(bf16[24,16,384]{2,1,0:T(8,128)(2,1)S(1)} %multiply_convert_fusion.15), channel_id=1, source_target_pairs={{0,8},{8,16},{16,24},{1,9},{9,17},{17,25},{2,10},{10,18},{18,26},{... | collective-permute-start | bytes 884744 | tf_op jit(solution)/shard_map/while/body/eval_jaxpr/ppermute | solution.py:28
  209.0 16.5 %collective-permute-start = (bf16[3,16,384]{2,1,0:T(8,128)(2,1)S(1)}, bf16[3,16,384]{2,1,0:T(8,128)(2,1)S(1)}, u32[]{:S(2)}, u32[]{:S(2)}) collective-permute-start(bf16[3,16,384]{2,1,0:T(8,128)(2,1)S(1)} %get-tuple-element.1573), channel_id=1, source_target_pairs={{4,0},{5,1},{6,2},{7,3},{12,8},{13,9},{14,10},{15,11},{20,16},{21,... | collective-permute-start | bytes 110600 | tf_op jit(solution)/shard_map/while/body/eval_jaxpr/ppermute | solution.py:20
  210.3 15.2 %collective-permute-start.1 = (bf16[3,16,384]{2,1,0:T(8,128)(2,1)S(1)}, bf16[3,16,384]{2,1,0:T(8,128)(2,1)S(1)}, u32[]{:S(2)}, u32[]{:S(2)}) collective-permute-start(bf16[3,16,384]{2,1,0:T(8,128)(2,1)S(1)} %get-tuple-element.1574), channel_id=1, source_target_pairs={{0,4},{1,5},{2,6},{3,7},{8,12},{9,13},{10,14},{11,15},{16,20},{17,... | collective-permute-start | bytes 110600 | tf_op jit(solution)/shard_map/while/body/eval_jaxpr/ppermute | solution.py:17
  236.1 11.4 %collective-permute-start.2 = (bf16[24,16,384]{2,1,0:T(8,128)(2,1)S(1)}, bf16[24,16,384]{2,1,0:T(8,128)(2,1)S(1)}, u32[]{:S(2)}, u32[]{:S(2)}) collective-permute-start(bf16[24,16,384]{2,1,0:T(8,128)(2,1)S(1)} %multiply_convert_fusion.15), channel_id=1, source_target_pairs={{0,8},{8,16},{16,24},{1,9},{9,17},{17,25},{2,10},{10,18},{18,26},{... | collective-permute-start | bytes 884744 | tf_op jit(solution)/shard_map/while/body/eval_jaxpr/ppermute | solution.py:28
  248.3 9.9 %copy-start.87 = (f32[1,384]{1,0:T(1,128)S(1)}, f32[1,384]{1,0:T(1,128)}, u32[]{:S(2)}) copy-start(f32[1,384]{1,0:T(1,128)} %get-tuple-element.1945) | copy-start | bytes 4612 | tf_op jit(solution)/shard_map/while
  248.3 9.9 %copy-start.97 = (bf16[1536,384]{1,0:T(8,128)(2,1)S(1)}, bf16[1536,384]{1,0:T(8,128)(2,1)}, u32[]{:S(2)}) copy-start(bf16[1536,384]{1,0:T(8,128)(2,1)} %get-tuple-element.1942) | copy-start | bytes 3538948 | tf_op jit(solution)/shard_map/while
  271.3 20.9 %collective-permute-start.3 = (bf16[3,16,384]{2,1,0:T(8,128)(2,1)}, bf16[3,16,384]{2,1,0:T(8,128)(2,1)}, u32[]{:S(2)}, u32[]{:S(2)}) collective-permute-start(bf16[3,16,384]{2,1,0:T(8,128)(2,1)} %get-tuple-element.1666), channel_id=1, source_target_pairs={{4,0},{5,1},{6,2},{7,3},{12,8},{13,9},{14,10},{15,11},{20,16},{21,... | collective-permute-start | bytes 110600 | tf_op jit(solution)/shard_map/while/body/eval_jaxpr/ppermute | solution.py:20
  272.6 19.6 %collective-permute-start.4 = (bf16[3,16,384]{2,1,0:T(8,128)(2,1)}, bf16[3,16,384]{2,1,0:T(8,128)(2,1)}, u32[]{:S(2)}, u32[]{:S(2)}) collective-permute-start(bf16[3,16,384]{2,1,0:T(8,128)(2,1)} %get-tuple-element.1667), channel_id=1, source_target_pairs={{0,4},{1,5},{2,6},{3,7},{8,12},{9,13},{10,14},{11,15},{16,20},{17,... | collective-permute-start | bytes 110600 | tf_op jit(solution)/shard_map/while/body/eval_jaxpr/ppermute | solution.py:17
  293.4 18.8 %copy-start.85 = (f32[384]{0:T(512)S(1)}, f32[384]{0:T(512)}, u32[]{:S(2)}) copy-start(f32[384]{0:T(512)} %get-tuple-element.1766) | copy-start | bytes 4612 | tf_op jit(solution)/shard_map/while
  293.4 19.0 %copy-start.27 = (f32[49,384]{1,0:T(8,128)S(1)}, f32[49,384]{1,0:T(8,128)}, u32[]{:S(2)}) copy-start(f32[49,384]{1,0:T(8,128)} %get-tuple-element.1895) | copy-start | bytes 225796 | tf_op jit(solution)/shard_map/while
  298.5 14.0 %collective-permute-start.5 = (bf16[24,16,384]{2,1,0:T(8,128)(2,1)S(1)}, bf16[24,16,384]{2,1,0:T(8,128)(2,1)S(1)}, u32[]{:S(2)}, u32[]{:S(2)}) collective-permute-start(bf16[24,16,384]{2,1,0:T(8,128)(2,1)S(1)} %fusion.416), channel_id=1, source_target_pairs={{8,0},{16,8},{24,16},{9,1},{17,9},{25,17},{10,2},{18,10},{26,18},{... | collective-permute-start | bytes 884744 | tf_op jit(solution)/shard_map/while/body/eval_jaxpr/ppermute | solution.py:28
  313.1 9.9 %copy-start.87 = (f32[1,384]{1,0:T(1,128)S(1)}, f32[1,384]{1,0:T(1,128)}, u32[]{:S(2)}) copy-start(f32[1,384]{1,0:T(1,128)} %get-tuple-element.1945) | copy-start | bytes 4612 | tf_op jit(solution)/shard_map/while
  313.1 9.9 %copy-start.97 = (bf16[1536,384]{1,0:T(8,128)(2,1)S(1)}, bf16[1536,384]{1,0:T(8,128)(2,1)}, u32[]{:S(2)}) copy-start(bf16[1536,384]{1,0:T(8,128)(2,1)} %get-tuple-element.1942) | copy-start | bytes 3538948 | tf_op jit(solution)/shard_map/while
  336.1 20.9 %collective-permute-start.3 = (bf16[3,16,384]{2,1,0:T(8,128)(2,1)}, bf16[3,16,384]{2,1,0:T(8,128)(2,1)}, u32[]{:S(2)}, u32[]{:S(2)}) collective-permute-start(bf16[3,16,384]{2,1,0:T(8,128)(2,1)} %get-tuple-element.1666), channel_id=1, source_target_pairs={{4,0},{5,1},{6,2},{7,3},{12,8},{13,9},{14,10},{15,11},{20,16},{21,... | collective-permute-start | bytes 110600 | tf_op jit(solution)/shard_map/while/body/eval_jaxpr/ppermute | solution.py:20
  337.3 19.6 %collective-permute-start.4 = (bf16[3,16,384]{2,1,0:T(8,128)(2,1)}, bf16[3,16,384]{2,1,0:T(8,128)(2,1)}, u32[]{:S(2)}, u32[]{:S(2)}) collective-permute-start(bf16[3,16,384]{2,1,0:T(8,128)(2,1)} %get-tuple-element.1667), channel_id=1, source_target_pairs={{0,4},{1,5},{2,6},{3,7},{8,12},{9,13},{10,14},{11,15},{16,20},{17,... | collective-permute-start | bytes 110600 | tf_op jit(solution)/shard_map/while/body/eval_jaxpr/ppermute | solution.py:17
  358.1 8.1 %copy-start.46 = (f32[384]{0:T(512)S(1)}, f32[384]{0:T(512)}, u32[]{:S(2)}) copy-start(f32[384]{0:T(512)} %get-tuple-element.1741) | copy-start | bytes 4612 | tf_op jit(solution)/shard_map/while
  358.2 8.1 %copy-start.45 = (f32[384]{0:T(512)S(1)}, f32[384]{0:T(512)}, u32[]{:S(2)}) copy-start(f32[384]{0:T(512)} %get-tuple-element.1743) | copy-start | bytes 4612 | tf_op jit(solution)/shard_map/while
  358.2 8.1 %copy-start.44 = (f32[384]{0:T(512)S(1)}, f32[384]{0:T(512)}, u32[]{:S(2)}) copy-start(f32[384]{0:T(512)} %get-tuple-element.1744) | copy-start | bytes 4612 | tf_op jit(solution)/shard_map/while
  358.2 8.2 %copy-start.43 = (f32[384]{0:T(512)S(1)}, f32[384]{0:T(512)}, u32[]{:S(2)}) copy-start(f32[384]{0:T(512)} %get-tuple-element.1745) | copy-start | bytes 4612 | tf_op jit(solution)/shard_map/while
  358.2 19.5 %copy-start.85 = (f32[384]{0:T(512)S(1)}, f32[384]{0:T(512)}, u32[]{:S(2)}) copy-start(f32[384]{0:T(512)} %get-tuple-element.1766) | copy-start | bytes 4612 | tf_op jit(solution)/shard_map/while
  358.2 19.7 %copy-start.27 = (f32[49,384]{1,0:T(8,128)S(1)}, f32[49,384]{1,0:T(8,128)}, u32[]{:S(2)}) copy-start(f32[49,384]{1,0:T(8,128)} %get-tuple-element.1895) | copy-start | bytes 225796 | tf_op jit(solution)/shard_map/while
  363.3 14.7 %collective-permute-start.5 = (bf16[24,16,384]{2,1,0:T(8,128)(2,1)S(1)}, bf16[24,16,384]{2,1,0:T(8,128)(2,1)S(1)}, u32[]{:S(2)}, u32[]{:S(2)}) collective-permute-start(bf16[24,16,384]{2,1,0:T(8,128)(2,1)S(1)} %fusion.416), channel_id=1, source_target_pairs={{8,0},{16,8},{24,16},{9,1},{17,9},{25,17},{10,2},{18,10},{26,18},{... | collective-permute-start | bytes 884744 | tf_op jit(solution)/shard_map/while/body/eval_jaxpr/ppermute | solution.py:28
  378.6 9.9 %copy-start.87 = (f32[1,384]{1,0:T(1,128)S(1)}, f32[1,384]{1,0:T(1,128)}, u32[]{:S(2)}) copy-start(f32[1,384]{1,0:T(1,128)} %get-tuple-element.1945) | copy-start | bytes 4612 | tf_op jit(solution)/shard_map/while
  378.6 9.9 %copy-start.97 = (bf16[1536,384]{1,0:T(8,128)(2,1)S(1)}, bf16[1536,384]{1,0:T(8,128)(2,1)}, u32[]{:S(2)}) copy-start(bf16[1536,384]{1,0:T(8,128)(2,1)} %get-tuple-element.1942) | copy-start | bytes 3538948 | tf_op jit(solution)/shard_map/while
  401.5 20.9 %collective-permute-start.3 = (bf16[3,16,384]{2,1,0:T(8,128)(2,1)}, bf16[3,16,384]{2,1,0:T(8,128)(2,1)}, u32[]{:S(2)}, u32[]{:S(2)}) collective-permute-start(bf16[3,16,384]{2,1,0:T(8,128)(2,1)} %get-tuple-element.1666), channel_id=1, source_target_pairs={{4,0},{5,1},{6,2},{7,3},{12,8},{13,9},{14,10},{15,11},{20,16},{21,... | collective-permute-start | bytes 110600 | tf_op jit(solution)/shard_map/while/body/eval_jaxpr/ppermute | solution.py:20
  402.8 19.6 %collective-permute-start.4 = (bf16[3,16,384]{2,1,0:T(8,128)(2,1)}, bf16[3,16,384]{2,1,0:T(8,128)(2,1)}, u32[]{:S(2)}, u32[]{:S(2)}) collective-permute-start(bf16[3,16,384]{2,1,0:T(8,128)(2,1)} %get-tuple-element.1667), channel_id=1, source_target_pairs={{0,4},{1,5},{2,6},{3,7},{8,12},{9,13},{10,14},{11,15},{16,20},{17,... | collective-permute-start | bytes 110600 | tf_op jit(solution)/shard_map/while/body/eval_jaxpr/ppermute | solution.py:17
  423.6 8.1 %copy-start.45 = (f32[384]{0:T(512)S(1)}, f32[384]{0:T(512)}, u32[]{:S(2)}) copy-start(f32[384]{0:T(512)} %get-tuple-element.1743) | copy-start | bytes 4612 | tf_op jit(solution)/shard_map/while
  423.6 8.1 %copy-start.44 = (f32[384]{0:T(512)S(1)}, f32[384]{0:T(512)}, u32[]{:S(2)}) copy-start(f32[384]{0:T(512)} %get-tuple-element.1744) | copy-start | bytes 4612 | tf_op jit(solution)/shard_map/while
  423.6 8.2 %copy-start.43 = (f32[384]{0:T(512)S(1)}, f32[384]{0:T(512)}, u32[]{:S(2)}) copy-start(f32[384]{0:T(512)} %get-tuple-element.1745) | copy-start | bytes 4612 | tf_op jit(solution)/shard_map/while
  423.7 19.5 %copy-start.85 = (f32[384]{0:T(512)S(1)}, f32[384]{0:T(512)}, u32[]{:S(2)}) copy-start(f32[384]{0:T(512)} %get-tuple-element.1766) | copy-start | bytes 4612 | tf_op jit(solution)/shard_map/while
  423.7 19.7 %copy-start.27 = (f32[49,384]{1,0:T(8,128)S(1)}, f32[49,384]{1,0:T(8,128)}, u32[]{:S(2)}) copy-start(f32[49,384]{1,0:T(8,128)} %get-tuple-element.1895) | copy-start | bytes 225796 | tf_op jit(solution)/shard_map/while
  428.7 14.7 %collective-permute-start.5 = (bf16[24,16,384]{2,1,0:T(8,128)(2,1)S(1)}, bf16[24,16,384]{2,1,0:T(8,128)(2,1)S(1)}, u32[]{:S(2)}, u32[]{:S(2)}) collective-permute-start(bf16[24,16,384]{2,1,0:T(8,128)(2,1)S(1)} %fusion.416), channel_id=1, source_target_pairs={{8,0},{16,8},{24,16},{9,1},{17,9},{25,17},{10,2},{18,10},{26,18},{... | collective-permute-start | bytes 884744 | tf_op jit(solution)/shard_map/while/body/eval_jaxpr/ppermute | solution.py:28
  444.1 9.9 %copy-start.87 = (f32[1,384]{1,0:T(1,128)S(1)}, f32[1,384]{1,0:T(1,128)}, u32[]{:S(2)}) copy-start(f32[1,384]{1,0:T(1,128)} %get-tuple-element.1945) | copy-start | bytes 4612 | tf_op jit(solution)/shard_map/while
  444.1 9.9 %copy-start.97 = (bf16[1536,384]{1,0:T(8,128)(2,1)S(1)}, bf16[1536,384]{1,0:T(8,128)(2,1)}, u32[]{:S(2)}) copy-start(bf16[1536,384]{1,0:T(8,128)(2,1)} %get-tuple-element.1942) | copy-start | bytes 3538948 | tf_op jit(solution)/shard_map/while
  467.0 21.5 %collective-permute-start.3 = (bf16[3,16,384]{2,1,0:T(8,128)(2,1)}, bf16[3,16,384]{2,1,0:T(8,128)(2,1)}, u32[]{:S(2)}, u32[]{:S(2)}) collective-permute-start(bf16[3,16,384]{2,1,0:T(8,128)(2,1)} %get-tuple-element.1666), channel_id=1, source_target_pairs={{4,0},{5,1},{6,2},{7,3},{12,8},{13,9},{14,10},{15,11},{20,16},{21,... | collective-permute-start | bytes 110600 | tf_op jit(solution)/shard_map/while/body/eval_jaxpr/ppermute | solution.py:20
  468.3 20.2 %collective-permute-start.4 = (bf16[3,16,384]{2,1,0:T(8,128)(2,1)}, bf16[3,16,384]{2,1,0:T(8,128)(2,1)}, u32[]{:S(2)}, u32[]{:S(2)}) collective-permute-start(bf16[3,16,384]{2,1,0:T(8,128)(2,1)} %get-tuple-element.1667), channel_id=1, source_target_pairs={{0,4},{1,5},{2,6},{3,7},{8,12},{9,13},{10,14},{11,15},{16,20},{17,... | collective-permute-start | bytes 110600 | tf_op jit(solution)/shard_map/while/body/eval_jaxpr/ppermute | solution.py:17
  489.7 8.1 %copy-start.45 = (f32[384]{0:T(512)S(1)}, f32[384]{0:T(512)}, u32[]{:S(2)}) copy-start(f32[384]{0:T(512)} %get-tuple-element.1743) | copy-start | bytes 4612 | tf_op jit(solution)/shard_map/while
  489.8 8.1 %copy-start.44 = (f32[384]{0:T(512)S(1)}, f32[384]{0:T(512)}, u32[]{:S(2)}) copy-start(f32[384]{0:T(512)} %get-tuple-element.1744) | copy-start | bytes 4612 | tf_op jit(solution)/shard_map/while
  489.8 8.2 %copy-start.43 = (f32[384]{0:T(512)S(1)}, f32[384]{0:T(512)}, u32[]{:S(2)}) copy-start(f32[384]{0:T(512)} %get-tuple-element.1745) | copy-start | bytes 4612 | tf_op jit(solution)/shard_map/while
  489.8 19.5 %copy-start.85 = (f32[384]{0:T(512)S(1)}, f32[384]{0:T(512)}, u32[]{:S(2)}) copy-start(f32[384]{0:T(512)} %get-tuple-element.1766) | copy-start | bytes 4612 | tf_op jit(solution)/shard_map/while
  489.8 19.7 %copy-start.27 = (f32[49,384]{1,0:T(8,128)S(1)}, f32[49,384]{1,0:T(8,128)}, u32[]{:S(2)}) copy-start(f32[49,384]{1,0:T(8,128)} %get-tuple-element.1895) | copy-start | bytes 225796 | tf_op jit(solution)/shard_map/while
  494.9 14.7 %collective-permute-start.5 = (bf16[24,16,384]{2,1,0:T(8,128)(2,1)S(1)}, bf16[24,16,384]{2,1,0:T(8,128)(2,1)S(1)}, u32[]{:S(2)}, u32[]{:S(2)}) collective-permute-start(bf16[24,16,384]{2,1,0:T(8,128)(2,1)S(1)} %fusion.416), channel_id=1, source_target_pairs={{8,0},{16,8},{24,16},{9,1},{17,9},{25,17},{10,2},{18,10},{26,18},{... | collective-permute-start | bytes 884744 | tf_op jit(solution)/shard_map/while/body/eval_jaxpr/ppermute | solution.py:28
  510.2 9.9 %copy-start.87 = (f32[1,384]{1,0:T(1,128)S(1)}, f32[1,384]{1,0:T(1,128)}, u32[]{:S(2)}) copy-start(f32[1,384]{1,0:T(1,128)} %get-tuple-element.1945) | copy-start | bytes 4612 | tf_op jit(solution)/shard_map/while
  510.2 9.9 %copy-start.97 = (bf16[1536,384]{1,0:T(8,128)(2,1)S(1)}, bf16[1536,384]{1,0:T(8,128)(2,1)}, u32[]{:S(2)}) copy-start(bf16[1536,384]{1,0:T(8,128)(2,1)} %get-tuple-element.1942) | copy-start | bytes 3538948 | tf_op jit(solution)/shard_map/while
  533.1 21.5 %collective-permute-start.3 = (bf16[3,16,384]{2,1,0:T(8,128)(2,1)}, bf16[3,16,384]{2,1,0:T(8,128)(2,1)}, u32[]{:S(2)}, u32[]{:S(2)}) collective-permute-start(bf16[3,16,384]{2,1,0:T(8,128)(2,1)} %get-tuple-element.1666), channel_id=1, source_target_pairs={{4,0},{5,1},{6,2},{7,3},{12,8},{13,9},{14,10},{15,11},{20,16},{21,... | collective-permute-start | bytes 110600 | tf_op jit(solution)/shard_map/while/body/eval_jaxpr/ppermute | solution.py:20
  534.4 20.2 %collective-permute-start.4 = (bf16[3,16,384]{2,1,0:T(8,128)(2,1)}, bf16[3,16,384]{2,1,0:T(8,128)(2,1)}, u32[]{:S(2)}, u32[]{:S(2)}) collective-permute-start(bf16[3,16,384]{2,1,0:T(8,128)(2,1)} %get-tuple-element.1667), channel_id=1, source_target_pairs={{0,4},{1,5},{2,6},{3,7},{8,12},{9,13},{10,14},{11,15},{16,20},{17,... | collective-permute-start | bytes 110600 | tf_op jit(solution)/shard_map/while/body/eval_jaxpr/ppermute | solution.py:17
  555.9 8.1 %copy-start.45 = (f32[384]{0:T(512)S(1)}, f32[384]{0:T(512)}, u32[]{:S(2)}) copy-start(f32[384]{0:T(512)} %get-tuple-element.1743) | copy-start | bytes 4612 | tf_op jit(solution)/shard_map/while
  555.9 8.1 %copy-start.44 = (f32[384]{0:T(512)S(1)}, f32[384]{0:T(512)}, u32[]{:S(2)}) copy-start(f32[384]{0:T(512)} %get-tuple-element.1744) | copy-start | bytes 4612 | tf_op jit(solution)/shard_map/while
  555.9 8.2 %copy-start.43 = (f32[384]{0:T(512)S(1)}, f32[384]{0:T(512)}, u32[]{:S(2)}) copy-start(f32[384]{0:T(512)} %get-tuple-element.1745) | copy-start | bytes 4612 | tf_op jit(solution)/shard_map/while
  555.9 19.5 %copy-start.85 = (f32[384]{0:T(512)S(1)}, f32[384]{0:T(512)}, u32[]{:S(2)}) copy-start(f32[384]{0:T(512)} %get-tuple-element.1766) | copy-start | bytes 4612 | tf_op jit(solution)/shard_map/while
  555.9 19.7 %copy-start.27 = (f32[49,384]{1,0:T(8,128)S(1)}, f32[49,384]{1,0:T(8,128)}, u32[]{:S(2)}) copy-start(f32[49,384]{1,0:T(8,128)} %get-tuple-element.1895) | copy-start | bytes 225796 | tf_op jit(solution)/shard_map/while
  561.0 14.7 %collective-permute-start.5 = (bf16[24,16,384]{2,1,0:T(8,128)(2,1)S(1)}, bf16[24,16,384]{2,1,0:T(8,128)(2,1)S(1)}, u32[]{:S(2)}, u32[]{:S(2)}) collective-permute-start(bf16[24,16,384]{2,1,0:T(8,128)(2,1)S(1)} %fusion.416), channel_id=1, source_target_pairs={{8,0},{16,8},{24,16},{9,1},{17,9},{25,17},{10,2},{18,10},{26,18},{... | collective-permute-start | bytes 884744 | tf_op jit(solution)/shard_map/while/body/eval_jaxpr/ppermute | solution.py:28
  (443 other events, 1757.2 us)
Sparse Core Ops, SparseCore 0:
  576.5 119.0 all-reduce.6
where the time goes:
time: 716 us; the launch traced here: 707 us
  local copies, waits for them, and re-layouts  217 us (30%)
  other arithmetic  176 us (25%)
  waiting for transfers between devices  100 us (14%)
  starting transfers between devices  81.2 us (11%)
  matrix products  55.4 us (8%)
  loops' own time  34.7 us (5%)
  blocking collectives  28.8 us (4%)
  between operations  14.1 us (2%)
    psum x1, waiting for transfers between devices, body(): lax.psum((totals[0], totals[1], totals[2], totals[3], totals[4], totals[5...  88 us
    another operation x250, local copies, waits for them, and re-layouts, block_backward_second(): return (grad_in, jnp.stack(taps))  58.2 us
    ppermute x10, starting transfers between devices, extended(): lax.ppermute(lax.slice_in_dim(block, block.shape[dim] - width, None, axis...  36.3 us
    while x940, local copies, waits for them, and re-layouts  32.4 us
    ppermute x10, starting transfers between devices, shifted(): lax.ppermute(value, axis, [(source, source + steps) for source in range(l...  32 us
    psum x1, blocking collectives, body(): lax.psum((totals[0], totals[1], totals[2], totals[3], totals[4], totals[5...  28.8 us
    reduce_sum x5, other arithmetic, block_forward(): centred = conv - jnp.mean(conv, axis=-1, keepdims=True)  27 us
    reduce_sum x15, other arithmetic, block_backward_second(): jnp.sum(field[i:i + row_count, j:j + col_count] * grad_conv, axis=(0, 1))  26.8 us
  transfers between devices with their start and end apart: 31, of which 6 were waited for; matrix products, arithmetic and copies ran while one was open for 29% of the time, Pallas kernels for 0%

commit v1 on v0

--- a/solution.py
+++ b/solution.py
@@ -215,10 +215,10 @@
     factor = 1.0 / math.sqrt(
         lax.axis_size("dp") * slot_count * lax.axis_size("rows") * row_count * col_count
     )
-    summed = lax.psum(
-        (totals[0], totals[1], totals[2], totals[3], totals[4], totals[5], totals[6]),
-        ("rows", "dp"),
-    )
+    half = lax.psum(
+        (totals[0], totals[1], totals[2], totals[3], totals[4], totals[5], totals[6]), "dp"
+    )
+    summed = lax.psum(half, "rows")
     finished = tuple(((part * factor).astype(jnp.bfloat16) for part in summed))
     return (
         finished[0][None],

time: 716 us -> 813 us (1.14)
  waiting for transfers between devices: 100 us -> 206 us
  blocking collectives: 28.8 us -> 19.5 us
    psum x1, waiting for transfers between devices: 88 us -> 184 us  [body(): lax.psum((totals[0], totals[1], totals[2], totals[3], totals[4], totals[5...]
    psum x1, blocking collectives: 28.8 us -> 16.2 us  [body(): lax.psum((totals[0], totals[1], totals[2], totals[3], totals[4], totals[5...]
    psum x0 -> x1, waiting for transfers between devices: none -> 9.32 us  [body(): summed = lax.psum(half, 'rows')]
  transfers between devices with their start and end apart: 31 -> 32, of which waited for: 6 -> 7; matrix products, arithmetic and copies ran while one was open for 29% -> 26% of each run, Pallas kernels for 0% -> 0%
where the time goes in v1:
time: 813 us; the launch traced here: 804 us
  local copies, waits for them, and re-layouts  217 us (27%)
  waiting for transfers between devices  206 us (25%)
  other arithmetic  176 us (22%)
  starting transfers between devices  81.3 us (10%)
  matrix products  55.4 us (7%)
  loops' own time  34.7 us (4%)
  blocking collectives  19.5 us (2%)
  between operations  14.1 us (2%)
    psum x1, waiting for transfers between devices, body(): lax.psum((totals[0], totals[1], totals[2], totals[3], totals[4], totals[5...  184 us
    another operation x250, local copies, waits for them, and re-layouts, block_backward_second(): return (grad_in, jnp.stack(taps))  58.2 us
    ppermute x10, starting transfers between devices, extended(): lax.ppermute(lax.slice_in_dim(block, block.shape[dim] - width, None, axis...  36.3 us
    while x940, local copies, waits for them, and re-layouts  32.4 us
    ppermute x10, starting transfers between devices, shifted(): lax.ppermute(value, axis, [(source, source + steps) for source in range(l...  32 us
    reduce_sum x5, other arithmetic, block_forward(): centred = conv - jnp.mean(conv, axis=-1, keepdims=True)  27 us
    reduce_sum x15, other arithmetic, block_backward_second(): jnp.sum(field[i:i + row_count, j:j + col_count] * grad_conv, axis=(0, 1))  26.8 us
    convert_element_type x5, other arithmetic, block_backward_second(): grad_in = (row_mask * (grad_res + total)).astype(jnp.bfloat16)  25.2 us
  transfers between devices with their start and end apart: 32, of which 7 were waited for; matrix products, arithmetic and copies ran while one was open for 26% of the time, Pallas kernels for 0%

profile of v1, /device:TPU:0, one launch (start us, length us, event | category | flops | bytes accessed | tf_op | source)
XLA Modules:
  0.0 803.8 jit_solution(6374721394736260511)
XLA Ops:
  10.1 2.7 broadcast_in_dim.122
  17.4 230.1 %while.58 = (s32[]{:T(128)}, bf16[24,16,384]{2,1,0:T(8,128)(2,1)S(1)}, bf16[2,30,16,384]{3,2,1,0:T(8,128)(2,1)}, f32[2,24,16,384]{3,2,1,0:T(8,128)}, f32[2,24,16...) while((s32[]{:T(128)}, ...), condition=%wide.region_5.6_spmd.clone, body=%wide.region_0.5_spmd.clone.sunk | while | flops 930707456 | bytes 118534944 | solution.py:184
  26.7 3.0 collective-permute-start.1
  35.1 1.9 constant_dynamic-slice_fusion.12
  42.0 5.4 fusion.394
  52.5 5.1 collective-permute-start.2
  61.0 2.4 collective-permute-done.2
  72.7 3.0 collective-permute-start.1
  81.2 1.9 constant_dynamic-slice_fusion.12
  88.0 5.4 fusion.394
  98.6 4.7 collective-permute-start.2
  106.6 2.4 collective-permute-done.2
  118.3 3.0 collective-permute-start.1
  126.8 1.9 constant_dynamic-slice_fusion.12
  133.6 5.4 fusion.394
  144.2 4.7 collective-permute-start.2
  152.2 2.4 collective-permute-done.2
  163.9 3.0 collective-permute-start.1
  172.3 1.9 constant_dynamic-slice_fusion.12
  179.2 5.4 fusion.394
  189.8 5.5 collective-permute-start.2
  198.6 2.4 collective-permute-done.2
  210.3 3.0 collective-permute-start.1
  218.7 1.9 constant_dynamic-slice_fusion.12
  225.6 5.4 fusion.394
  236.1 5.6 collective-permute-start.2
  245.1 2.4 collective-permute-done.2
  248.1 328.2 %while.59 = (s32[]{:T(128)}, bf16[24,16,384]{2,1,0:T(8,128)(2,1)S(1)}, f32[49,384]{1,0:T(8,128)}, f32[3,384]{1,0:T(4,128)}, f32[1,384]{1,0:T(1,128)}, /*index=5*...) while((s32[]{:T(128)}, ...), condition=%wide.region_64.65_spmd.clone, body=%wide.region_6.64_spmd.clone.sunk | while | flops 1859761920 | bytes 116535416 | solution.py:214
  256.1 1.9 fusion.408
  258.3 3.3 fusion.410
  265.3 2.4 fusion.413
  267.7 2.2 fusion.414
  272.6 4.2 collective-permute-start.4
  285.7 3.4 fusion.423
  293.4 5.0 fusion.416
  323.0 3.3 fusion.410
  330.1 2.4 fusion.413
  332.5 2.2 fusion.414
  337.3 4.2 collective-permute-start.4
  350.5 3.4 fusion.423
  358.2 5.0 fusion.416
  388.5 3.3 fusion.410
  395.6 2.4 fusion.413
  398.0 2.2 fusion.414
  402.8 4.2 collective-permute-start.4
  416.0 3.4 fusion.423
  423.7 5.0 fusion.416
  454.0 3.3 fusion.410
  461.0 2.4 fusion.413
  463.4 2.2 fusion.414
  468.3 4.2 collective-permute-start.4
  482.1 3.4 fusion.423
  489.8 5.0 fusion.416
  520.1 3.3 fusion.410
  527.2 2.4 fusion.413
  529.6 2.2 fusion.414
  534.4 4.2 collective-permute-start.4
  548.2 3.4 fusion.423
  555.9 5.0 fusion.416
  576.4 184.4 %all-reduce.10.cloned.1.call-done = (f32[49,384]{1,0:T(8,128)}, f32[384,1536]{1,0:T(8,128)}, f32[1536,384]{1,0:T(8,128)}) async-done(((f32[49,384]{1,0:T(8,128)}, f32[384,1536]{1,0:T(8,128)}, f32[1536,384]{1,0:T(8,128)}), (f32[49,384]{1,0:T(8,128)}, f32[384,1536]{1,0:T(8,128)}, f32[1536,384]{1,0:T(8,128)})) %all-reduce.10.cloned.1.call-update) | async-done | bytes 4793872 | tf_op jit(solution)/shard_map/psum | solution.py:218
  761.5 16.2 %all-reduce.3 = (f32[3,384]{1,0:T(4,128)S(1)}, f32[1,384]{1,0:T(1,128)S(1)}, f32[1,384]{1,0:T(1,128)S(1)}, f32[1,1536]{1,0:T(1,128)S(1)}) all-reduce(f32[3,384]{1,0:T(4,128)S(1)} %copy-done.39, f32[1,384]{1,0:T(1,128)S(1)} %copy-done.90, f32[1,384]{1,0:T(1,128)S(1)} %copy-done.91, ...), channel_id=1, replica_groups=mesh['section'=4,'rows'=2,'dp'=4] {'dp'}, use_global_device_ids=true, to_apply=%region_67.68 | all-reduce | flops 3456 | bytes 27648 | tf_op jit(solution)/shard_map/psum | solution.py:218
  777.7 3.3 all-reduce.5
  782.8 9.3 %all-reduce.12.cloned.1.call-done = (f32[49,384]{1,0:T(8,128)}, f32[384,1536]{1,0:T(8,128)}, f32[1536,384]{1,0:T(8,128)}) async-done(((f32[49,384]{1,0:T(8,128)}, f32[384,1536]{1,0:T(8,128)}, f32[1536,384]{1,0:T(8,128)}), (f32[49,384]{1,0:T(8,128)}, f32[384,1536]{1,0:T(8,128)}, f32[1536,384]{1,0:T(8,128)})) %all-reduce.12.cloned.1.call-update) | async-done | bytes 4793872 | tf_op jit(solution)/shard_map/psum | solution.py:221
  792.1 3.0 fusion.334
  (1588 shorter events, 341.7 us)
Async XLA Ops:
  7.2 753.6 %all-reduce.10.cloned.1.call-start = ((), (), s32[]{:S(2)}) async-start(), calls=%async_computation | async-start | bytes 9609216 | tf_op jit(solution)/shard_map/psum | solution.py:218
  25.4 16.5 %collective-permute-start = (bf16[3,16,384]{2,1,0:T(8,128)(2,1)S(1)}, bf16[3,16,384]{2,1,0:T(8,128)(2,1)S(1)}, u32[]{:S(2)}, u32[]{:S(2)}) collective-permute-start(bf16[3,16,384]{2,1,0:T(8,128)(2,1)S(1)} %get-tuple-element.1580), channel_id=1, source_target_pairs={{4,0},{5,1},{6,2},{7,3},{12,8},{13,9},{14,10},{15,11},{20,16},{21,... | collective-permute-start | bytes 110600 | tf_op jit(solution)/shard_map/while/body/eval_jaxpr/ppermute | solution.py:20
  26.7 15.2 %collective-permute-start.1 = (bf16[3,16,384]{2,1,0:T(8,128)(2,1)S(1)}, bf16[3,16,384]{2,1,0:T(8,128)(2,1)S(1)}, u32[]{:S(2)}, u32[]{:S(2)}) collective-permute-start(bf16[3,16,384]{2,1,0:T(8,128)(2,1)S(1)} %get-tuple-element.1581), channel_id=1, source_target_pairs={{0,4},{1,5},{2,6},{3,7},{8,12},{9,13},{10,14},{11,15},{16,20},{17,... | collective-permute-start | bytes 110600 | tf_op jit(solution)/shard_map/while/body/eval_jaxpr/ppermute | solution.py:17
  52.5 10.9 %collective-permute-start.2 = (bf16[24,16,384]{2,1,0:T(8,128)(2,1)S(1)}, bf16[24,16,384]{2,1,0:T(8,128)(2,1)S(1)}, u32[]{:S(2)}, u32[]{:S(2)}) collective-permute-start(bf16[24,16,384]{2,1,0:T(8,128)(2,1)S(1)} %multiply_convert_fusion.15), channel_id=1, source_target_pairs={{0,8},{8,16},{16,24},{1,9},{9,17},{17,25},{2,10},{10,18},{18,26},{... | collective-permute-start | bytes 884744 | tf_op jit(solution)/shard_map/while/body/eval_jaxpr/ppermute | solution.py:28
  71.4 16.5 %collective-permute-start = (bf16[3,16,384]{2,1,0:T(8,128)(2,1)S(1)}, bf16[3,16,384]{2,1,0:T(8,128)(2,1)S(1)}, u32[]{:S(2)}, u32[]{:S(2)}) collective-permute-start(bf16[3,16,384]{2,1,0:T(8,128)(2,1)S(1)} %get-tuple-element.1580), channel_id=1, source_target_pairs={{4,0},{5,1},{6,2},{7,3},{12,8},{13,9},{14,10},{15,11},{20,16},{21,... | collective-permute-start | bytes 110600 | tf_op jit(solution)/shard_map/while/body/eval_jaxpr/ppermute | solution.py:20
  72.7 15.2 %collective-permute-start.1 = (bf16[3,16,384]{2,1,0:T(8,128)(2,1)S(1)}, bf16[3,16,384]{2,1,0:T(8,128)(2,1)S(1)}, u32[]{:S(2)}, u32[]{:S(2)}) collective-permute-start(bf16[3,16,384]{2,1,0:T(8,128)(2,1)S(1)} %get-tuple-element.1581), channel_id=1, source_target_pairs={{0,4},{1,5},{2,6},{3,7},{8,12},{9,13},{10,14},{11,15},{16,20},{17,... | collective-permute-start | bytes 110600 | tf_op jit(solution)/shard_map/while/body/eval_jaxpr/ppermute | solution.py:17
  98.6 10.5 %collective-permute-start.2 = (bf16[24,16,384]{2,1,0:T(8,128)(2,1)S(1)}, bf16[24,16,384]{2,1,0:T(8,128)(2,1)S(1)}, u32[]{:S(2)}, u32[]{:S(2)}) collective-permute-start(bf16[24,16,384]{2,1,0:T(8,128)(2,1)S(1)} %multiply_convert_fusion.15), channel_id=1, source_target_pairs={{0,8},{8,16},{16,24},{1,9},{9,17},{17,25},{2,10},{10,18},{18,26},{... | collective-permute-start | bytes 884744 | tf_op jit(solution)/shard_map/while/body/eval_jaxpr/ppermute | solution.py:28
  117.0 16.5 %collective-permute-start = (bf16[3,16,384]{2,1,0:T(8,128)(2,1)S(1)}, bf16[3,16,384]{2,1,0:T(8,128)(2,1)S(1)}, u32[]{:S(2)}, u32[]{:S(2)}) collective-permute-start(bf16[3,16,384]{2,1,0:T(8,128)(2,1)S(1)} %get-tuple-element.1580), channel_id=1, source_target_pairs={{4,0},{5,1},{6,2},{7,3},{12,8},{13,9},{14,10},{15,11},{20,16},{21,... | collective-permute-start | bytes 110600 | tf_op jit(solution)/shard_map/while/body/eval_jaxpr/ppermute | solution.py:20
  118.3 15.2 %collective-permute-start.1 = (bf16[3,16,384]{2,1,0:T(8,128)(2,1)S(1)}, bf16[3,16,384]{2,1,0:T(8,128)(2,1)S(1)}, u32[]{:S(2)}, u32[]{:S(2)}) collective-permute-start(bf16[3,16,384]{2,1,0:T(8,128)(2,1)S(1)} %get-tuple-element.1581), channel_id=1, source_target_pairs={{0,4},{1,5},{2,6},{3,7},{8,12},{9,13},{10,14},{11,15},{16,20},{17,... | collective-permute-start | bytes 110600 | tf_op jit(solution)/shard_map/while/body/eval_jaxpr/ppermute | solution.py:17
  144.2 10.5 %collective-permute-start.2 = (bf16[24,16,384]{2,1,0:T(8,128)(2,1)S(1)}, bf16[24,16,384]{2,1,0:T(8,128)(2,1)S(1)}, u32[]{:S(2)}, u32[]{:S(2)}) collective-permute-start(bf16[24,16,384]{2,1,0:T(8,128)(2,1)S(1)} %multiply_convert_fusion.15), channel_id=1, source_target_pairs={{0,8},{8,16},{16,24},{1,9},{9,17},{17,25},{2,10},{10,18},{18,26},{... | collective-permute-start | bytes 884744 | tf_op jit(solution)/shard_map/while/body/eval_jaxpr/ppermute | solution.py:28
  162.6 16.5 %collective-permute-start = (bf16[3,16,384]{2,1,0:T(8,128)(2,1)S(1)}, bf16[3,16,384]{2,1,0:T(8,128)(2,1)S(1)}, u32[]{:S(2)}, u32[]{:S(2)}) collective-permute-start(bf16[3,16,384]{2,1,0:T(8,128)(2,1)S(1)} %get-tuple-element.1580), channel_id=1, source_target_pairs={{4,0},{5,1},{6,2},{7,3},{12,8},{13,9},{14,10},{15,11},{20,16},{21,... | collective-permute-start | bytes 110600 | tf_op jit(solution)/shard_map/while/body/eval_jaxpr/ppermute | solution.py:20
  163.9 15.2 %collective-permute-start.1 = (bf16[3,16,384]{2,1,0:T(8,128)(2,1)S(1)}, bf16[3,16,384]{2,1,0:T(8,128)(2,1)S(1)}, u32[]{:S(2)}, u32[]{:S(2)}) collective-permute-start(bf16[3,16,384]{2,1,0:T(8,128)(2,1)S(1)} %get-tuple-element.1581), channel_id=1, source_target_pairs={{0,4},{1,5},{2,6},{3,7},{8,12},{9,13},{10,14},{11,15},{16,20},{17,... | collective-permute-start | bytes 110600 | tf_op jit(solution)/shard_map/while/body/eval_jaxpr/ppermute | solution.py:17
  189.8 11.3 %collective-permute-start.2 = (bf16[24,16,384]{2,1,0:T(8,128)(2,1)S(1)}, bf16[24,16,384]{2,1,0:T(8,128)(2,1)S(1)}, u32[]{:S(2)}, u32[]{:S(2)}) collective-permute-start(bf16[24,16,384]{2,1,0:T(8,128)(2,1)S(1)} %multiply_convert_fusion.15), channel_id=1, source_target_pairs={{0,8},{8,16},{16,24},{1,9},{9,17},{17,25},{2,10},{10,18},{18,26},{... | collective-permute-start | bytes 884744 | tf_op jit(solution)/shard_map/while/body/eval_jaxpr/ppermute | solution.py:28
  209.0 16.5 %collective-permute-start = (bf16[3,16,384]{2,1,0:T(8,128)(2,1)S(1)}, bf16[3,16,384]{2,1,0:T(8,128)(2,1)S(1)}, u32[]{:S(2)}, u32[]{:S(2)}) collective-permute-start(bf16[3,16,384]{2,1,0:T(8,128)(2,1)S(1)} %get-tuple-element.1580), channel_id=1, source_target_pairs={{4,0},{5,1},{6,2},{7,3},{12,8},{13,9},{14,10},{15,11},{20,16},{21,... | collective-permute-start | bytes 110600 | tf_op jit(solution)/shard_map/while/body/eval_jaxpr/ppermute | solution.py:20
  210.3 15.2 %collective-permute-start.1 = (bf16[3,16,384]{2,1,0:T(8,128)(2,1)S(1)}, bf16[3,16,384]{2,1,0:T(8,128)(2,1)S(1)}, u32[]{:S(2)}, u32[]{:S(2)}) collective-permute-start(bf16[3,16,384]{2,1,0:T(8,128)(2,1)S(1)} %get-tuple-element.1581), channel_id=1, source_target_pairs={{0,4},{1,5},{2,6},{3,7},{8,12},{9,13},{10,14},{11,15},{16,20},{17,... | collective-permute-start | bytes 110600 | tf_op jit(solution)/shard_map/while/body/eval_jaxpr/ppermute | solution.py:17
  236.1 11.4 %collective-permute-start.2 = (bf16[24,16,384]{2,1,0:T(8,128)(2,1)S(1)}, bf16[24,16,384]{2,1,0:T(8,128)(2,1)S(1)}, u32[]{:S(2)}, u32[]{:S(2)}) collective-permute-start(bf16[24,16,384]{2,1,0:T(8,128)(2,1)S(1)} %multiply_convert_fusion.15), channel_id=1, source_target_pairs={{0,8},{8,16},{16,24},{1,9},{9,17},{17,25},{2,10},{10,18},{18,26},{... | collective-permute-start | bytes 884744 | tf_op jit(solution)/shard_map/while/body/eval_jaxpr/ppermute | solution.py:28
  248.3 9.9 %copy-start.87 = (f32[1,384]{1,0:T(1,128)S(1)}, f32[1,384]{1,0:T(1,128)}, u32[]{:S(2)}) copy-start(f32[1,384]{1,0:T(1,128)} %get-tuple-element.1952) | copy-start | bytes 4612 | tf_op jit(solution)/shard_map/while
  248.3 9.9 %copy-start.97 = (bf16[1536,384]{1,0:T(8,128)(2,1)S(1)}, bf16[1536,384]{1,0:T(8,128)(2,1)}, u32[]{:S(2)}) copy-start(bf16[1536,384]{1,0:T(8,128)(2,1)} %get-tuple-element.1949) | copy-start | bytes 3538948 | tf_op jit(solution)/shard_map/while
  271.3 20.9 %collective-permute-start.3 = (bf16[3,16,384]{2,1,0:T(8,128)(2,1)}, bf16[3,16,384]{2,1,0:T(8,128)(2,1)}, u32[]{:S(2)}, u32[]{:S(2)}) collective-permute-start(bf16[3,16,384]{2,1,0:T(8,128)(2,1)} %get-tuple-element.1673), channel_id=1, source_target_pairs={{4,0},{5,1},{6,2},{7,3},{12,8},{13,9},{14,10},{15,11},{20,16},{21,... | collective-permute-start | bytes 110600 | tf_op jit(solution)/shard_map/while/body/eval_jaxpr/ppermute | solution.py:20
  272.6 19.6 %collective-permute-start.4 = (bf16[3,16,384]{2,1,0:T(8,128)(2,1)}, bf16[3,16,384]{2,1,0:T(8,128)(2,1)}, u32[]{:S(2)}, u32[]{:S(2)}) collective-permute-start(bf16[3,16,384]{2,1,0:T(8,128)(2,1)} %get-tuple-element.1674), channel_id=1, source_target_pairs={{0,4},{1,5},{2,6},{3,7},{8,12},{9,13},{10,14},{11,15},{16,20},{17,... | collective-permute-start | bytes 110600 | tf_op jit(solution)/shard_map/while/body/eval_jaxpr/ppermute | solution.py:17
  293.4 18.8 %copy-start.85 = (f32[384]{0:T(512)S(1)}, f32[384]{0:T(512)}, u32[]{:S(2)}) copy-start(f32[384]{0:T(512)} %get-tuple-element.1773) | copy-start | bytes 4612 | tf_op jit(solution)/shard_map/while
  293.4 19.0 %copy-start.27 = (f32[49,384]{1,0:T(8,128)S(1)}, f32[49,384]{1,0:T(8,128)}, u32[]{:S(2)}) copy-start(f32[49,384]{1,0:T(8,128)} %get-tuple-element.1902) | copy-start | bytes 225796 | tf_op jit(solution)/shard_map/while
  298.5 14.0 %collective-permute-start.5 = (bf16[24,16,384]{2,1,0:T(8,128)(2,1)S(1)}, bf16[24,16,384]{2,1,0:T(8,128)(2,1)S(1)}, u32[]{:S(2)}, u32[]{:S(2)}) collective-permute-start(bf16[24,16,384]{2,1,0:T(8,128)(2,1)S(1)} %fusion.416), channel_id=1, source_target_pairs={{8,0},{16,8},{24,16},{9,1},{17,9},{25,17},{10,2},{18,10},{26,18},{... | collective-permute-start | bytes 884744 | tf_op jit(solution)/shard_map/while/body/eval_jaxpr/ppermute | solution.py:28
  313.1 9.9 %copy-start.87 = (f32[1,384]{1,0:T(1,128)S(1)}, f32[1,384]{1,0:T(1,128)}, u32[]{:S(2)}) copy-start(f32[1,384]{1,0:T(1,128)} %get-tuple-element.1952) | copy-start | bytes 4612 | tf_op jit(solution)/shard_map/while
  313.1 9.9 %copy-start.97 = (bf16[1536,384]{1,0:T(8,128)(2,1)S(1)}, bf16[1536,384]{1,0:T(8,128)(2,1)}, u32[]{:S(2)}) copy-start(bf16[1536,384]{1,0:T(8,128)(2,1)} %get-tuple-element.1949) | copy-start | bytes 3538948 | tf_op jit(solution)/shard_map/while
  336.1 20.9 %collective-permute-start.3 = (bf16[3,16,384]{2,1,0:T(8,128)(2,1)}, bf16[3,16,384]{2,1,0:T(8,128)(2,1)}, u32[]{:S(2)}, u32[]{:S(2)}) collective-permute-start(bf16[3,16,384]{2,1,0:T(8,128)(2,1)} %get-tuple-element.1673), channel_id=1, source_target_pairs={{4,0},{5,1},{6,2},{7,3},{12,8},{13,9},{14,10},{15,11},{20,16},{21,... | collective-permute-start | bytes 110600 | tf_op jit(solution)/shard_map/while/body/eval_jaxpr/ppermute | solution.py:20
  337.3 19.6 %collective-permute-start.4 = (bf16[3,16,384]{2,1,0:T(8,128)(2,1)}, bf16[3,16,384]{2,1,0:T(8,128)(2,1)}, u32[]{:S(2)}, u32[]{:S(2)}) collective-permute-start(bf16[3,16,384]{2,1,0:T(8,128)(2,1)} %get-tuple-element.1674), channel_id=1, source_target_pairs={{0,4},{1,5},{2,6},{3,7},{8,12},{9,13},{10,14},{11,15},{16,20},{17,... | collective-permute-start | bytes 110600 | tf_op jit(solution)/shard_map/while/body/eval_jaxpr/ppermute | solution.py:17
  358.2 8.1 %copy-start.45 = (f32[384]{0:T(512)S(1)}, f32[384]{0:T(512)}, u32[]{:S(2)}) copy-start(f32[384]{0:T(512)} %get-tuple-element.1750) | copy-start | bytes 4612 | tf_op jit(solution)/shard_map/while
  358.2 8.1 %copy-start.44 = (f32[384]{0:T(512)S(1)}, f32[384]{0:T(512)}, u32[]{:S(2)}) copy-start(f32[384]{0:T(512)} %get-tuple-element.1751) | copy-start | bytes 4612 | tf_op jit(solution)/shard_map/while
  358.2 8.2 %copy-start.43 = (f32[384]{0:T(512)S(1)}, f32[384]{0:T(512)}, u32[]{:S(2)}) copy-start(f32[384]{0:T(512)} %get-tuple-element.1752) | copy-start | bytes 4612 | tf_op jit(solution)/shard_map/while
  358.2 19.5 %copy-start.85 = (f32[384]{0:T(512)S(1)}, f32[384]{0:T(512)}, u32[]{:S(2)}) copy-start(f32[384]{0:T(512)} %get-tuple-element.1773) | copy-start | bytes 4612 | tf_op jit(solution)/shard_map/while
  358.2 19.7 %copy-start.27 = (f32[49,384]{1,0:T(8,128)S(1)}, f32[49,384]{1,0:T(8,128)}, u32[]{:S(2)}) copy-start(f32[49,384]{1,0:T(8,128)} %get-tuple-element.1902) | copy-start | bytes 225796 | tf_op jit(solution)/shard_map/while
  363.3 14.7 %collective-permute-start.5 = (bf16[24,16,384]{2,1,0:T(8,128)(2,1)S(1)}, bf16[24,16,384]{2,1,0:T(8,128)(2,1)S(1)}, u32[]{:S(2)}, u32[]{:S(2)}) collective-permute-start(bf16[24,16,384]{2,1,0:T(8,128)(2,1)S(1)} %fusion.416), channel_id=1, source_target_pairs={{8,0},{16,8},{24,16},{9,1},{17,9},{25,17},{10,2},{18,10},{26,18},{... | collective-permute-start | bytes 884744 | tf_op jit(solution)/shard_map/while/body/eval_jaxpr/ppermute | solution.py:28
  378.6 9.9 %copy-start.87 = (f32[1,384]{1,0:T(1,128)S(1)}, f32[1,384]{1,0:T(1,128)}, u32[]{:S(2)}) copy-start(f32[1,384]{1,0:T(1,128)} %get-tuple-element.1952) | copy-start | bytes 4612 | tf_op jit(solution)/shard_map/while
  378.6 9.9 %copy-start.97 = (bf16[1536,384]{1,0:T(8,128)(2,1)S(1)}, bf16[1536,384]{1,0:T(8,128)(2,1)}, u32[]{:S(2)}) copy-start(bf16[1536,384]{1,0:T(8,128)(2,1)} %get-tuple-element.1949) | copy-start | bytes 3538948 | tf_op jit(solution)/shard_map/while
  401.5 20.9 %collective-permute-start.3 = (bf16[3,16,384]{2,1,0:T(8,128)(2,1)}, bf16[3,16,384]{2,1,0:T(8,128)(2,1)}, u32[]{:S(2)}, u32[]{:S(2)}) collective-permute-start(bf16[3,16,384]{2,1,0:T(8,128)(2,1)} %get-tuple-element.1673), channel_id=1, source_target_pairs={{4,0},{5,1},{6,2},{7,3},{12,8},{13,9},{14,10},{15,11},{20,16},{21,... | collective-permute-start | bytes 110600 | tf_op jit(solution)/shard_map/while/body/eval_jaxpr/ppermute | solution.py:20
  402.8 19.6 %collective-permute-start.4 = (bf16[3,16,384]{2,1,0:T(8,128)(2,1)}, bf16[3,16,384]{2,1,0:T(8,128)(2,1)}, u32[]{:S(2)}, u32[]{:S(2)}) collective-permute-start(bf16[3,16,384]{2,1,0:T(8,128)(2,1)} %get-tuple-element.1674), channel_id=1, source_target_pairs={{0,4},{1,5},{2,6},{3,7},{8,12},{9,13},{10,14},{11,15},{16,20},{17,... | collective-permute-start | bytes 110600 | tf_op jit(solution)/shard_map/while/body/eval_jaxpr/ppermute | solution.py:17
  423.6 8.1 %copy-start.45 = (f32[384]{0:T(512)S(1)}, f32[384]{0:T(512)}, u32[]{:S(2)}) copy-start(f32[384]{0:T(512)} %get-tuple-element.1750) | copy-start | bytes 4612 | tf_op jit(solution)/shard_map/while
  423.6 8.1 %copy-start.44 = (f32[384]{0:T(512)S(1)}, f32[384]{0:T(512)}, u32[]{:S(2)}) copy-start(f32[384]{0:T(512)} %get-tuple-element.1751) | copy-start | bytes 4612 | tf_op jit(solution)/shard_map/while
  423.6 8.2 %copy-start.43 = (f32[384]{0:T(512)S(1)}, f32[384]{0:T(512)}, u32[]{:S(2)}) copy-start(f32[384]{0:T(512)} %get-tuple-element.1752) | copy-start | bytes 4612 | tf_op jit(solution)/shard_map/while
  423.7 19.5 %copy-start.85 = (f32[384]{0:T(512)S(1)}, f32[384]{0:T(512)}, u32[]{:S(2)}) copy-start(f32[384]{0:T(512)} %get-tuple-element.1773) | copy-start | bytes 4612 | tf_op jit(solution)/shard_map/while
  423.7 19.7 %copy-start.27 = (f32[49,384]{1,0:T(8,128)S(1)}, f32[49,384]{1,0:T(8,128)}, u32[]{:S(2)}) copy-start(f32[49,384]{1,0:T(8,128)} %get-tuple-element.1902) | copy-start | bytes 225796 | tf_op jit(solution)/shard_map/while
  428.7 14.7 %collective-permute-start.5 = (bf16[24,16,384]{2,1,0:T(8,128)(2,1)S(1)}, bf16[24,16,384]{2,1,0:T(8,128)(2,1)S(1)}, u32[]{:S(2)}, u32[]{:S(2)}) collective-permute-start(bf16[24,16,384]{2,1,0:T(8,128)(2,1)S(1)} %fusion.416), channel_id=1, source_target_pairs={{8,0},{16,8},{24,16},{9,1},{17,9},{25,17},{10,2},{18,10},{26,18},{... | collective-permute-start | bytes 884744 | tf_op jit(solution)/shard_map/while/body/eval_jaxpr/ppermute | solution.py:28
  444.1 9.9 %copy-start.87 = (f32[1,384]{1,0:T(1,128)S(1)}, f32[1,384]{1,0:T(1,128)}, u32[]{:S(2)}) copy-start(f32[1,384]{1,0:T(1,128)} %get-tuple-element.1952) | copy-start | bytes 4612 | tf_op jit(solution)/shard_map/while
  444.1 9.9 %copy-start.97 = (bf16[1536,384]{1,0:T(8,128)(2,1)S(1)}, bf16[1536,384]{1,0:T(8,128)(2,1)}, u32[]{:S(2)}) copy-start(bf16[1536,384]{1,0:T(8,128)(2,1)} %get-tuple-element.1949) | copy-start | bytes 3538948 | tf_op jit(solution)/shard_map/while
  467.0 21.5 %collective-permute-start.3 = (bf16[3,16,384]{2,1,0:T(8,128)(2,1)}, bf16[3,16,384]{2,1,0:T(8,128)(2,1)}, u32[]{:S(2)}, u32[]{:S(2)}) collective-permute-start(bf16[3,16,384]{2,1,0:T(8,128)(2,1)} %get-tuple-element.1673), channel_id=1, source_target_pairs={{4,0},{5,1},{6,2},{7,3},{12,8},{13,9},{14,10},{15,11},{20,16},{21,... | collective-permute-start | bytes 110600 | tf_op jit(solution)/shard_map/while/body/eval_jaxpr/ppermute | solution.py:20
  468.3 20.2 %collective-permute-start.4 = (bf16[3,16,384]{2,1,0:T(8,128)(2,1)}, bf16[3,16,384]{2,1,0:T(8,128)(2,1)}, u32[]{:S(2)}, u32[]{:S(2)}) collective-permute-start(bf16[3,16,384]{2,1,0:T(8,128)(2,1)} %get-tuple-element.1674), channel_id=1, source_target_pairs={{0,4},{1,5},{2,6},{3,7},{8,12},{9,13},{10,14},{11,15},{16,20},{17,... | collective-permute-start | bytes 110600 | tf_op jit(solution)/shard_map/while/body/eval_jaxpr/ppermute | solution.py:17
  489.7 8.1 %copy-start.45 = (f32[384]{0:T(512)S(1)}, f32[384]{0:T(512)}, u32[]{:S(2)}) copy-start(f32[384]{0:T(512)} %get-tuple-element.1750) | copy-start | bytes 4612 | tf_op jit(solution)/shard_map/while
  489.8 8.1 %copy-start.44 = (f32[384]{0:T(512)S(1)}, f32[384]{0:T(512)}, u32[]{:S(2)}) copy-start(f32[384]{0:T(512)} %get-tuple-element.1751) | copy-start | bytes 4612 | tf_op jit(solution)/shard_map/while
  489.8 8.2 %copy-start.43 = (f32[384]{0:T(512)S(1)}, f32[384]{0:T(512)}, u32[]{:S(2)}) copy-start(f32[384]{0:T(512)} %get-tuple-element.1752) | copy-start | bytes 4612 | tf_op jit(solution)/shard_map/while
  489.8 19.5 %copy-start.85 = (f32[384]{0:T(512)S(1)}, f32[384]{0:T(512)}, u32[]{:S(2)}) copy-start(f32[384]{0:T(512)} %get-tuple-element.1773) | copy-start | bytes 4612 | tf_op jit(solution)/shard_map/while
  489.8 19.7 %copy-start.27 = (f32[49,384]{1,0:T(8,128)S(1)}, f32[49,384]{1,0:T(8,128)}, u32[]{:S(2)}) copy-start(f32[49,384]{1,0:T(8,128)} %get-tuple-element.1902) | copy-start | bytes 225796 | tf_op jit(solution)/shard_map/while
  494.9 14.7 %collective-permute-start.5 = (bf16[24,16,384]{2,1,0:T(8,128)(2,1)S(1)}, bf16[24,16,384]{2,1,0:T(8,128)(2,1)S(1)}, u32[]{:S(2)}, u32[]{:S(2)}) collective-permute-start(bf16[24,16,384]{2,1,0:T(8,128)(2,1)S(1)} %fusion.416), channel_id=1, source_target_pairs={{8,0},{16,8},{24,16},{9,1},{17,9},{25,17},{10,2},{18,10},{26,18},{... | collective-permute-start | bytes 884744 | tf_op jit(solution)/shard_map/while/body/eval_jaxpr/ppermute | solution.py:28
  510.2 9.9 %copy-start.87 = (f32[1,384]{1,0:T(1,128)S(1)}, f32[1,384]{1,0:T(1,128)}, u32[]{:S(2)}) copy-start(f32[1,384]{1,0:T(1,128)} %get-tuple-element.1952) | copy-start | bytes 4612 | tf_op jit(solution)/shard_map/while
  510.2 9.9 %copy-start.97 = (bf16[1536,384]{1,0:T(8,128)(2,1)S(1)}, bf16[1536,384]{1,0:T(8,128)(2,1)}, u32[]{:S(2)}) copy-start(bf16[1536,384]{1,0:T(8,128)(2,1)} %get-tuple-element.1949) | copy-start | bytes 3538948 | tf_op jit(solution)/shard_map/while
  533.1 21.5 %collective-permute-start.3 = (bf16[3,16,384]{2,1,0:T(8,128)(2,1)}, bf16[3,16,384]{2,1,0:T(8,128)(2,1)}, u32[]{:S(2)}, u32[]{:S(2)}) collective-permute-start(bf16[3,16,384]{2,1,0:T(8,128)(2,1)} %get-tuple-element.1673), channel_id=1, source_target_pairs={{4,0},{5,1},{6,2},{7,3},{12,8},{13,9},{14,10},{15,11},{20,16},{21,... | collective-permute-start | bytes 110600 | tf_op jit(solution)/shard_map/while/body/eval_jaxpr/ppermute | solution.py:20
  534.4 20.2 %collective-permute-start.4 = (bf16[3,16,384]{2,1,0:T(8,128)(2,1)}, bf16[3,16,384]{2,1,0:T(8,128)(2,1)}, u32[]{:S(2)}, u32[]{:S(2)}) collective-permute-start(bf16[3,16,384]{2,1,0:T(8,128)(2,1)} %get-tuple-element.1674), channel_id=1, source_target_pairs={{0,4},{1,5},{2,6},{3,7},{8,12},{9,13},{10,14},{11,15},{16,20},{17,... | collective-permute-start | bytes 110600 | tf_op jit(solution)/shard_map/while/body/eval_jaxpr/ppermute | solution.py:17
  555.9 8.1 %copy-start.45 = (f32[384]{0:T(512)S(1)}, f32[384]{0:T(512)}, u32[]{:S(2)}) copy-start(f32[384]{0:T(512)} %get-tuple-element.1750) | copy-start | bytes 4612 | tf_op jit(solution)/shard_map/while
  555.9 8.1 %copy-start.44 = (f32[384]{0:T(512)S(1)}, f32[384]{0:T(512)}, u32[]{:S(2)}) copy-start(f32[384]{0:T(512)} %get-tuple-element.1751) | copy-start | bytes 4612 | tf_op jit(solution)/shard_map/while
  555.9 8.2 %copy-start.43 = (f32[384]{0:T(512)S(1)}, f32[384]{0:T(512)}, u32[]{:S(2)}) copy-start(f32[384]{0:T(512)} %get-tuple-element.1752) | copy-start | bytes 4612 | tf_op jit(solution)/shard_map/while
  555.9 19.5 %copy-start.85 = (f32[384]{0:T(512)S(1)}, f32[384]{0:T(512)}, u32[]{:S(2)}) copy-start(f32[384]{0:T(512)} %get-tuple-element.1773) | copy-start | bytes 4612 | tf_op jit(solution)/shard_map/while
  555.9 19.7 %copy-start.27 = (f32[49,384]{1,0:T(8,128)S(1)}, f32[49,384]{1,0:T(8,128)}, u32[]{:S(2)}) copy-start(f32[49,384]{1,0:T(8,128)} %get-tuple-element.1902) | copy-start | bytes 225796 | tf_op jit(solution)/shard_map/while
  561.0 14.7 %collective-permute-start.5 = (bf16[24,16,384]{2,1,0:T(8,128)(2,1)S(1)}, bf16[24,16,384]{2,1,0:T(8,128)(2,1)S(1)}, u32[]{:S(2)}, u32[]{:S(2)}) collective-permute-start(bf16[24,16,384]{2,1,0:T(8,128)(2,1)S(1)} %fusion.416), channel_id=1, source_target_pairs={{8,0},{16,8},{24,16},{9,1},{17,9},{25,17},{10,2},{18,10},{26,18},{... | collective-permute-start | bytes 884744 | tf_op jit(solution)/shard_map/while/body/eval_jaxpr/ppermute | solution.py:28
  576.3 215.8 %all-reduce.12.cloned.1.call-start = ((), (), s32[]{:S(2)}) async-start(), calls=%async_computation.1 | async-start | bytes 9609216 | tf_op jit(solution)/shard_map/psum | solution.py:221
  (444 other events, 1765.3 us)
Sparse Core Ops, SparseCore 0:
  576.4 184.2 all-reduce.9
  763.5 28.5 all-reduce.11
